TPU v7x, 32 devices: a whole 2x2x4 slice. The times are simulated.
32 devices in a mesh: dir: 4 (over x, core), tb: 8 (over z, y).
Axes of the slice: x: 2, y: 2, z: 4, core: 2. Of those that a mesh axis runs over, the one named last changes fastest.
Arguments:
- visibilities: bfloat16 [8192, 128], P('tb'), may hold values from -6 to 6
- uv_coords: bfloat16 [2, 8192], P(None, 'tb'), may hold values from -32 to 32
- comp_lm: float32 [2, 12288], P(None, 'dir'), may hold values from -0.25 to 0.25
- spectra: bfloat16 [2, 12288, 128], P(None, 'dir'), may hold values from -0.1875 to 0.1875
- ridge_weight: float32 [128], replicated, may hold values from 32 to 512
- assignment: int32 [12288], P('dir'), may hold values from 0 to 3071, as said below
- peel_order: int32 [12], P('dir'), may hold values from 0 to 2, as said below
- block_tile: int32 [256, 1], P('tb'), may hold values from 0 to 7; in each aligned block of 32 rows (0 to 31, 32 to 63, ...) at most 8 rows name the same one
Outputs:
- residual: bfloat16 [8192, 128], P('tb')
- subgrids: float32 [8, 2, 1024, 128], P('tb', None, 'dir')
Inputs may be any that keep to these rules, and one draw needn't show every extreme that they name: `assignment`: each owner's 3 * 1024 entries are a permutation of its local component numbers. `peel_order`: each owner's 3 entries are a permutation of its directions. `block_tile`: among the 32 blocks of one index of tb no tile is named more than 8 times; every tile is named by some block of the whole array.
All inputs are finite; a program needn't handle non-finite values.
Results may differ from a plain program's by a relative error of at most 0.0064.
Values may be sent and summed in bfloat16 or wider, within the bound.
A program may use at most 64 MiB of HBM per device.

v0:
```python
import functools
import math

import jax
import jax.numpy as jnp
from jax import lax
from jax.experimental import pallas as pl
from jax.experimental.pallas import tpu as pltpu
from jax.sharding import PartitionSpec as P

NCOMP = 1024
GRID = 32
DIR_DEV = 3
ITERS = 4
BB = 32
GB = 128
ROWS_DEV = 1024
PIX = 1024

MESH = pl.DeviceIdType.MESH
F32 = jnp.float32
BF16 = jnp.bfloat16
LANES = 128
CHUNK = 256
SUB = 32

SIN_FIT = (4.4428795675460835, -7.307816684491791, 3.5977741780872416, -0.7911993921613704)
COS_FIT = (1.414204014809076, -6.977637323456295, 5.715187874756718, -1.728213892223522)


def horner(square, fit):
    total = fit[-1]
    for coefficient in fit[-2::-1]:
        total = total * square + coefficient
    return total


def turn_cos_sin(turns):
    part = turns - jnp.round(turns)
    square = part * part
    half_sin = part * horner(square, SIN_FIT)
    half_cos = horner(square, COS_FIT)
    return (1.0 - half_sin * half_sin).astype(BF16), (half_sin * half_cos).astype(BF16)


def kernel(
    owners,
    peers,
    slots,
    vis_ref,
    uv_ref,
    lm_ref,
    spec_ref,
    ridge_ref,
    entry_ref,
    tile_ref,
    peel_ref,
    resid_ref,
    grid_ref,
    masked,
    lm_parts,
    coord_rows,
    block_row,
    block_of_ref,
    coords_out,
    turned_a,
    turned_b,
    acc,
    models_out,
    models_in,
    resid,
    rows_out,
    rows_in,
    coords_in,
    tables,
    m_send,
    m_recv,
    r_send,
    r_recv,
    d_send,
    d_recv,
    c_send,
    c_recv,
    index_sem,
):
    me_d = lax.axis_index("dir")
    me_t = lax.axis_index("tb")
    sample_rows, columns = vis_ref.shape
    comps = lm_ref.shape[1]
    group_rows = sample_rows // owners
    block_count = sample_rows // BB
    group_blocks = block_count // owners
    slot_rows = slots * BB

    barrier = pltpu.get_barrier_semaphore()
    for k in range(1, owners):
        pl.semaphore_signal(
            barrier, inc=1, device_id={"dir": lax.rem(me_d + k, owners)}, device_id_type=MESH
        )

    def greet(k, carry):
        pl.semaphore_signal(
            barrier, inc=1, device_id={"tb": lax.rem(me_t + k, peers)}, device_id_type=MESH
        )
        return carry

    lax.fori_loop(1, peers, greet, 0)
    pl.semaphore_wait(barrier, owners - 1 + peers - 1)

    slot_lanes = block_row.shape[1]
    tiles = jnp.broadcast_to(tile_ref[...], (slot_lanes, block_count))
    named_tile = jnp.where(
        lax.broadcasted_iota(jnp.int32, (slot_lanes, block_count), 0) == tiles, 1.0, 0.0
    )
    earlier = jnp.where(
        lax.broadcasted_iota(jnp.int32, (block_count, block_count), 0)
        < lax.broadcasted_iota(jnp.int32, (block_count, block_count), 1),
        1.0,
        0.0,
    )
    ranks = jnp.dot(named_tile.astype(BF16), earlier.astype(BF16), preferred_element_type=F32)
    slot = jnp.sum(ranks * named_tile, axis=0, keepdims=True).astype(jnp.int32)
    target = jnp.broadcast_to(tile_ref[...] * slots + slot, (slot_lanes, block_count))
    lane = lax.broadcasted_iota(jnp.int32, (slot_lanes, block_count), 0)
    taken = jnp.where(lane == target, 1.0, 0.0).astype(BF16)
    block_id = lax.broadcasted_iota(jnp.int32, (8, block_count), 1) - block_count
    picked = lax.dot_general(
        block_id.astype(F32).astype(BF16),
        taken,
        (((1,), (1,)), ((), ())),
        preferred_element_type=F32,
    )
    block_row[...] = picked[0:1, :].astype(jnp.int32) + block_count
    index_copy = pltpu.make_async_copy(block_row, block_of_ref, index_sem)
    index_copy.start()

    u_row = uv_ref[0:1, :].astype(F32)
    v_row = uv_ref[1:2, :].astype(F32)
    stacked = jnp.concatenate(
        [u_row] * 3 + [v_row] * 3 + [jnp.zeros((LANES - 6, sample_rows), F32)], axis=0
    )
    coord_rows[0:block_count] = (
        stacked.T.astype(BF16).reshape(block_count, BB, LANES)
    )
    coord_rows[block_count] = jnp.zeros((BB, LANES), BF16)

    parts = []
    for which in range(2):
        left = lm_ref[which : which + 1, :]
        for part in range(3):
            rounded = left.astype(BF16).astype(F32)
            parts.append(rounded)
            left = left - rounded
    parts.append(jnp.zeros((2, comps), F32))
    lm_parts[...] = jnp.concatenate(parts, axis=0).astype(BF16)

    strips = comps // LANES
    padded = -(-strips // 16) * 16
    named = jnp.concatenate([entry_ref[r : r + 1, :] for r in range(strips)], axis=1)
    places = []
    for direction in range(DIR_DEV):
        value = jnp.int32(0)
        for position in range(DIR_DEV):
            value = value + jnp.where(peel_ref[position] == direction, position, 0)
        places.append(jnp.full((1, comps // DIR_DEV), value, jnp.int32))
    place = jnp.concatenate(places, axis=1).astype(F32)
    low = lax.broadcasted_iota(jnp.int32, (LANES, comps), 0)
    high = lax.broadcasted_iota(jnp.int32, (padded, comps), 0)
    at_low = jnp.where(low == named % LANES, 1.0, 0.0).astype(BF16)
    at_high = jnp.where(high == named // LANES, place, 0.0).astype(BF16)
    positions = lax.dot_general(
        at_low, at_high, (((1,), (1,)), ((), ())), preferred_element_type=F32
    )
    for strip in range(strips):
        own = jnp.broadcast_to(positions[:, strip : strip + 1], (LANES, columns)).astype(BF16)
        span = pl.ds(strip * LANES, LANES)
        for part in range(2):
            values = spec_ref[part, span, :]
            for position in range(DIR_DEV):
                masked[part, span, position * columns : (position + 1) * columns] = jnp.where(
                    own == jnp.asarray(position, BF16), values, jnp.zeros_like(values)
                )

    def coords_copy(src, owner, to):
        return pltpu.make_async_remote_copy(
            src_ref=coords_out.at[src],
            dst_ref=coords_in.at[owner],
            send_sem=c_send.at[src],
            recv_sem=c_recv.at[owner],
            device_id={"tb": to},
            device_id_type=MESH,
        )

    index_copy.wait()

    def block_in(to, slot):
        block = block_of_ref[0, to * slots + slot]
        return jnp.minimum(jnp.maximum(block, 0), block_count)

    def send_coords(k, carry):
        to = lax.rem(me_t + k, peers)
        for slot in range(slots):
            coords_out[to, slot * BB : (slot + 1) * BB, :] = coord_rows[block_in(to, slot)]

        @pl.when(k < peers)
        def _():
            coords_copy(to, me_t, to).start()

        return carry

    lax.fori_loop(1, peers + 1, send_coords, 0)
    coords_in[me_t] = coords_out[me_t]

    def models_copy(group, owner, to):
        return pltpu.make_async_remote_copy(
            src_ref=models_out.at[group],
            dst_ref=models_in.at[owner],
            send_sem=m_send.at[group],
            recv_sem=m_recv.at[owner],
            device_id={"dir": to},
            device_id_type=MESH,
        )

    def predict_group(k, carry):
        group = lax.rem(me_d + k, owners)
        group_coords = coord_rows[pl.ds(group * group_blocks, group_blocks)]
        group_coords = group_coords.reshape(group_rows, LANES)[:, 0:8]
        chunks = comps // CHUNK
        buffers = (turned_a, turned_b)
        pieces = group_rows // SUB

        def spread_turns(chunk):
            return jnp.dot(
                group_coords,
                lm_parts[:, chunk * CHUNK : (chunk + 1) * CHUNK],
                preferred_element_type=F32,
            )

        def contract_chunk(chunk, part):
            return jnp.dot(
                buffers[chunk % 2][part],
                masked[part, chunk * CHUNK : (chunk + 1) * CHUNK, :],
                preferred_element_type=F32,
            )

        turns = spread_turns(0)
        for chunk in range(chunks):
            turned = buffers[chunk % 2]
            following = None
            for sub in range(pieces):
                rows = slice(sub * SUB, (sub + 1) * SUB)
                cos_part, sin_part = turn_cos_sin(turns[rows])
                turned[0, rows, :] = cos_part
                turned[1, rows, :] = sin_part
                if chunk > 0 and sub == 0:
                    update = contract_chunk(chunk - 1, 0)
                if chunk > 0 and sub == pieces // 2 - 1:
                    update = update + contract_chunk(chunk - 1, 1)
                    if chunk == 1:
                        acc[...] = update
                    else:
                        acc[...] += update
                if chunk + 1 < chunks and sub == pieces - 2:
                    following = spread_turns(chunk + 1)
            turns = following
        last = contract_chunk(chunks - 1, 0) + contract_chunk(chunks - 1, 1)
        final = (acc[...] + last).astype(BF16)

        @pl.when(k < owners)
        def _():
            models_out[group] = final
            models_copy(group, me_d, group).start()

        @pl.when(k == owners)
        def _():
            models_in[me_d] = final

        return carry

    lax.fori_loop(1, owners + 1, predict_group, 0)

    def wait_coords(k, carry):
        source = lax.rem(me_t + k, peers)
        coords_copy(source, source, source).wait()
        return carry

    lax.fori_loop(1, peers, wait_coords, 0)
    share = grid_ref.shape[1]
    pixel = me_d * share + lax.broadcasted_iota(jnp.int32, (share, LANES), 0)
    which = lax.broadcasted_iota(jnp.int32, (share, LANES), 1)
    pixel_xy = jnp.where(
        which == 0,
        (pixel // GRID - GRID // 2).astype(F32),
        jnp.where(which == 3, (pixel % GRID - GRID // 2).astype(F32), 0.0),
    )
    pixel_xy = (pixel_xy / (2.0 * GRID)).astype(BF16)

    def make_table(source, carry):
        turns = lax.dot_general(
            pixel_xy, coords_in[source], (((1,), (1,)), ((), ())), preferred_element_type=F32
        )
        cos_part, sin_part = turn_cos_sin(turns)
        tables[source, 0:share, :] = cos_part
        tables[source, share : 2 * share, :] = sin_part
        return carry

    lax.fori_loop(0, peers, make_table, 0)

    def wait_models(k, carry):
        source = lax.rem(me_d + k, owners)
        models_copy(source, source, source).wait()
        return carry

    lax.fori_loop(1, owners, wait_models, 0)

    gain_blocks = group_rows // GB
    first = me_d * group_rows
    ridge = jnp.broadcast_to(ridge_ref[...], (8, columns))
    lane = lax.broadcasted_iota(jnp.int32, (8, columns), 1)

    def over_rows(value):
        total = jnp.sum(jnp.sum(value, axis=0), axis=0, keepdims=True)
        return jnp.broadcast_to(total, (8, columns))

    def peel_owner(owner, remains):
        out = []
        for block in range(gain_blocks):
            rest = remains[block]
            for position in range(DIR_DEV):
                model = models_in[
                    owner,
                    block * GB : (block + 1) * GB,
                    position * columns : (position + 1) * columns,
                ].astype(F32)
                model = model.reshape(GB // 8, 8, columns)
                cross_sum = over_rows(rest * model)
                inverse = 1.0 / (over_rows(model * model) + ridge)
                gain = jnp.ones_like(cross_sum)
                for sweep in range(ITERS):
                    before = jnp.where(lane < 2, gain, pltpu.roll(gain, 2, 1))
                    after = jnp.where(
                        lane >= columns - 2, gain, pltpu.roll(gain, columns - 2, 1)
                    )
                    gain = (cross_sum + ridge * (0.5 * (before + after))) * inverse
                rest = rest - gain[None] * model
            out.append(rest.astype(BF16).astype(F32))
        return tuple(out)

    start = tuple(
        vis_ref[pl.ds(pl.multiple_of(first + block * GB, GB), GB), :]
        .astype(F32)
        .reshape(GB // 8, 8, columns)
        for block in range(gain_blocks)
    )
    done = lax.fori_loop(0, owners, peel_owner, start)
    per_gain = GB // BB
    for block in range(gain_blocks):
        resid[pl.ds(me_d * group_blocks + block * per_gain, per_gain)] = (
            done[block].reshape(per_gain, BB, columns).astype(BF16)
        )
    resid[block_count] = jnp.zeros((BB, columns), BF16)

    def resid_copy(group, sem, to):
        part = pl.ds(group * group_blocks, group_blocks)
        return pltpu.make_async_remote_copy(
            src_ref=resid.at[part],
            dst_ref=resid.at[part],
            send_sem=r_send.at[sem],
            recv_sem=r_recv.at[group],
            device_id={"dir": to},
            device_id_type=MESH,
        )

    for k in range(1, owners):
        to = lax.rem(me_d + k, owners)
        resid_copy(me_d, to, to).start()
    for k in range(1, owners):
        source = lax.rem(me_d + k, owners)
        resid_copy(source, source, source).wait_recv()

    def rows_copy(src, owner, to):
        return pltpu.make_async_remote_copy(
            src_ref=rows_out.at[src],
            dst_ref=rows_in.at[owner],
            send_sem=d_send.at[src],
            recv_sem=d_recv.at[owner],
            device_id={"tb": to},
            device_id_type=MESH,
        )

    def dispatch(k, carry):
        to = lax.rem(me_t + k, peers)
        for slot in range(slots):
            rows_out[to, slot * BB : (slot + 1) * BB, :] = resid[block_in(to, slot)]

        @pl.when(k < peers)
        def _():
            rows_copy(to, me_t, to).start()

        return carry

    lax.fori_loop(1, peers + 1, dispatch, 0)
    resid_ref[...] = resid[0:block_count].reshape(sample_rows, columns)

    grid_sum = jnp.dot(tables[me_t], rows_out[me_t], preferred_element_type=F32)

    def add_source(k, total):
        source = lax.rem(me_t + k, peers)
        rows_copy(source, source, source).wait_recv()
        return total + jnp.dot(tables[source], rows_in[source], preferred_element_type=F32)

    grid_sum = lax.fori_loop(1, peers, add_source, grid_sum)
    grid_ref[...] = (grid_sum * float(ROWS_DEV) ** (-0.5)).reshape(2, share, columns)

    for k in range(1, owners):
        to = lax.rem(me_d + k, owners)
        resid_copy(me_d, to, to).wait_send()

    def drain(k, carry):
        to = lax.rem(me_t + k, peers)
        rows_copy(to, me_t, to).wait_send()
        return carry

    lax.fori_loop(1, peers, drain, 0)


def finish(resid_ref, grid_ref, resid_out, grid_out, sem):
    copies = (
        pltpu.make_async_copy(resid_ref, resid_out, sem.at[0]),
        pltpu.make_async_copy(grid_ref, grid_out, sem.at[1]),
    )
    for copy in copies:
        copy.start()
    for copy in copies:
        copy.wait()


def local(
    owners,
    peers,
    visibilities,
    uv_coords,
    comp_lm,
    spectra,
    ridge_weight,
    assignment,
    peel_order,
    block_tile,
):
    sample_rows, columns = visibilities.shape
    comps = comp_lm.shape[1]
    block_count = sample_rows // BB
    slots = max(2, 2 * block_count // peers)
    share = PIX // owners

    slot_lanes = -(-peers * slots // LANES) * LANES
    vmem = pl.BlockSpec(memory_space=pltpu.VMEM)
    smem = pl.BlockSpec(memory_space=pltpu.SMEM)
    dma = pltpu.SemaphoreType.DMA
    residual, subgrid = pl.pallas_call(
        functools.partial(kernel, owners, peers, slots),
        out_shape=(
            jax.ShapeDtypeStruct((sample_rows, columns), BF16),
            jax.ShapeDtypeStruct((2, share, columns), F32),
        ),
        in_specs=[vmem] * 7 + [smem],
        out_specs=(vmem, vmem),
        scratch_shapes=[
            pltpu.VMEM((2, comps, DIR_DEV * columns), BF16),
            pltpu.VMEM((8, comps), BF16),
            pltpu.VMEM((block_count + 1, BB, LANES), BF16),
            pltpu.VMEM((1, slot_lanes), jnp.int32),
            pltpu.SMEM((1, slot_lanes), jnp.int32),
            pltpu.VMEM((peers, slots * BB, LANES), BF16),
            pltpu.VMEM((2, sample_rows // owners, CHUNK), BF16),
            pltpu.VMEM((2, sample_rows // owners, CHUNK), BF16),
            pltpu.VMEM((sample_rows // owners, DIR_DEV * columns), F32),
            pltpu.VMEM((owners, sample_rows // owners, DIR_DEV * columns), BF16),
            pltpu.VMEM((owners, sample_rows // owners, DIR_DEV * columns), BF16),
            pltpu.VMEM((block_count + 1, BB, columns), BF16),
            pltpu.VMEM((peers, slots * BB, columns), BF16),
            pltpu.VMEM((peers, slots * BB, columns), BF16),
            pltpu.VMEM((peers, slots * BB, LANES), BF16),
            pltpu.VMEM((peers, 2 * share, slots * BB), BF16),
            dma((owners,)),
            dma((owners,)),
            dma((owners,)),
            dma((owners,)),
            dma((peers,)),
            dma((peers,)),
            dma((peers,)),
            dma((peers,)),
            dma,
        ],
        compiler_params=pltpu.CompilerParams(
            collective_id=0, has_side_effects=True, vmem_limit_bytes=60 * 1024 * 1024
        ),
    )(
        visibilities,
        uv_coords,
        comp_lm,
        spectra,
        ridge_weight[None, :],
        assignment.reshape(comps // LANES, LANES),
        block_tile.reshape(1, block_count),
        peel_order,
    )
    anywhere = pl.BlockSpec(memory_space=pl.ANY)
    residual, subgrid = pl.pallas_call(
        finish,
        out_shape=(
            jax.ShapeDtypeStruct(residual.shape, residual.dtype),
            jax.ShapeDtypeStruct(subgrid.shape, subgrid.dtype),
        ),
        in_specs=[vmem] * 2,
        out_specs=(anywhere, anywhere),
        scratch_shapes=[dma((2,))],
    )(residual, subgrid)
    return residual, subgrid[None]


def solution(mesh):
    return jax.shard_map(
        functools.partial(local, mesh.shape["dir"], mesh.shape["tb"]),
        mesh=mesh,
        in_specs=(
            P("tb", None),
            P(None, "tb"),
            P(None, "dir"),
            P(None, "dir", None),
            P(),
            P("dir"),
            P("dir"),
            P("tb", None),
        ),
        out_specs=(P("tb", None), P("tb", None, "dir", None)),
        check_vma=False,
    )
```

profile of v0, /device:TPU:13, one launch (start us, length us, event | category | flops | bytes accessed | tf_op | source)
XLA Modules:
  0.0 49.0 jit_solution(2786233981317991042)
XLA Ops:
  0.6 46.5 %shard_map.95 = (bf16[1024,128]{1,0:T(8,128)(2,1)}, f32[2,256,128]{2,1,0:T(8,128)}) custom-call(bf16[1024,128]{1,0:T(8,128)(2,1)} %vis_ref.1, bf16[2,1024]{1,0:T(2,128)(2,1)} %uv_ref.1, f32[2,3072]{1,0:T(2,128)} %lm_ref.1, bf16[2,3072,128]{2,1,0:T(8,128)(2,1)} %spec_ref.1, f32[1,128]{1,0:T(1,128)} %bitcast.5, s32[24,128]{1,0:T(8,128)} %bitcast.4, ...), custom_call_target="tpu_custom_call" | custom-call | tf_op jit(solution)/shard_map/pallas_call | solution.py:460
  47.2 1.8 %shard_map.96 = (bf16[1024,128]{1,0:T(8,128)(2,1)}, f32[2,256,128]{2,1,0:T(8,128)}) custom-call(bf16[1024,128]{1,0:T(8,128)(2,1)} %get-tuple-element.6.resid_ref, f32[2,256,128]{2,1,0:T(8,128)} %get-tuple-element.7.grid_ref), custom_call_target="tpu_custom_call" | custom-call | tf_op jit(solution)/shard_map/pallas_call | solution.py:509
where the time goes:
time: 49.2 us; the launch traced here: 49 us
  Pallas kernels  48.4 us (98%)
  between operations  0.64 us (1%)
    pallas_call x1, Pallas kernels, local(): pl.pallas_call(functools.partial(kernel, owners, peers, slots), out_shape...  46.5 us
    pallas_call x1, Pallas kernels, local(): pl.pallas_call(finish, out_shape=(jax.ShapeDtypeStruct(residual.shape, re...  1.83 us

commit v1 on v0

--- a/solution.py
+++ b/solution.py
@@ -40,23 +40,25 @@
     square = part * part
     half_sin = part * horner(square, SIN_FIT)
     half_cos = horner(square, COS_FIT)
-    return (1.0 - half_sin * half_sin).astype(BF16), (half_sin * half_cos).astype(BF16)
+    return 1.0 - half_sin * half_sin, half_sin * half_cos
 
 
 def kernel(
     owners,
     peers,
     slots,
-    vis_ref,
     uv_ref,
     lm_ref,
-    spec_ref,
     ridge_ref,
     entry_ref,
     tile_ref,
     peel_ref,
+    vis_hbm,
+    spec_hbm,
     resid_ref,
     grid_ref,
+    vis_buf,
+    spec_buf,
     masked,
     lm_parts,
     coord_rows,
@@ -69,6 +71,7 @@
     models_out,
     models_in,
     resid,
+    own_rows,
     rows_out,
     rows_in,
     coords_in,
@@ -79,18 +82,32 @@
     r_recv,
     d_send,
     d_recv,
+    f_send,
+    f_recv,
     c_send,
     c_recv,
-    index_sem,
+    local_sem,
 ):
     me_d = lax.axis_index("dir")
     me_t = lax.axis_index("tb")
-    sample_rows, columns = vis_ref.shape
+    core = me_d % 2
+    partner = me_d + 1 - 2 * core
+    group_rows, columns = vis_buf.shape
+    sample_rows = group_rows * owners
     comps = lm_ref.shape[1]
-    group_rows = sample_rows // owners
     block_count = sample_rows // BB
     group_blocks = block_count // owners
     slot_rows = slots * BB
+    half_slots = slots // 2
+    half_rows = half_slots * BB
+    first = me_d * group_rows
+
+    spec_copy = pltpu.make_async_copy(spec_hbm, spec_buf, local_sem.at[0])
+    vis_copy = pltpu.make_async_copy(
+        vis_hbm.at[pl.ds(pl.multiple_of(first, group_rows), group_rows)], vis_buf, local_sem.at[1]
+    )
+    spec_copy.start()
+    vis_copy.start()
 
     barrier = pltpu.get_barrier_semaphore()
     for k in range(1, owners):
@@ -105,7 +122,6 @@
         return carry
 
     lax.fori_loop(1, peers, greet, 0)
-    pl.semaphore_wait(barrier, owners - 1 + peers - 1)
 
     slot_lanes = block_row.shape[1]
     tiles = jnp.broadcast_to(tile_ref[...], (slot_lanes, block_count))
@@ -131,18 +147,36 @@
         preferred_element_type=F32,
     )
     block_row[...] = picked[0:1, :].astype(jnp.int32) + block_count
-    index_copy = pltpu.make_async_copy(block_row, block_of_ref, index_sem)
+    index_copy = pltpu.make_async_copy(block_row, block_of_ref, local_sem.at[2])
     index_copy.start()
 
     u_row = uv_ref[0:1, :].astype(F32)
     v_row = uv_ref[1:2, :].astype(F32)
+    in_block = (
+        lax.broadcasted_iota(jnp.int32, (block_count, sample_rows), 1) // BB
+        == lax.broadcasted_iota(jnp.int32, (block_count, sample_rows), 0)
+    )
+    at_lane = jnp.where(
+        lax.broadcasted_iota(jnp.int32, (sample_rows, LANES), 0) % BB
+        == lax.broadcasted_iota(jnp.int32, (sample_rows, LANES), 1) % BB,
+        1.0,
+        0.0,
+    ).astype(BF16)
+    packed, side = coords_out.shape[1], coords_out.shape[1] // 2
+    spot = lax.broadcasted_iota(jnp.int32, (peers * packed, block_count), 0)
+    place_of = tile_ref[...] * packed + slot
+    sent = jnp.zeros((peers * packed, LANES), F32)
+    for which, row in enumerate((u_row, v_row)):
+        spread = jnp.where(in_block, jnp.broadcast_to(row, in_block.shape), 0.0).astype(BF16)
+        by_block = jnp.dot(spread, at_lane, preferred_element_type=F32).astype(BF16)
+        chosen = jnp.where(spot == place_of + which * side, 1.0, 0.0).astype(BF16)
+        sent = sent + jnp.dot(chosen, by_block, preferred_element_type=F32)
+    coords_out[...] = sent.astype(BF16).reshape(peers, packed, LANES)
+
     stacked = jnp.concatenate(
         [u_row] * 3 + [v_row] * 3 + [jnp.zeros((LANES - 6, sample_rows), F32)], axis=0
     )
-    coord_rows[0:block_count] = (
-        stacked.T.astype(BF16).reshape(block_count, BB, LANES)
-    )
-    coord_rows[block_count] = jnp.zeros((BB, LANES), BF16)
+    coord_rows[...] = stacked.T.astype(BF16)
 
     parts = []
     for which in range(2):
@@ -171,11 +205,12 @@
     positions = lax.dot_general(
         at_low, at_high, (((1,), (1,)), ((), ())), preferred_element_type=F32
     )
+    spec_copy.wait()
     for strip in range(strips):
         own = jnp.broadcast_to(positions[:, strip : strip + 1], (LANES, columns)).astype(BF16)
         span = pl.ds(strip * LANES, LANES)
         for part in range(2):
-            values = spec_ref[part, span, :]
+            values = spec_buf[part, span, :]
             for position in range(DIR_DEV):
                 masked[part, span, position * columns : (position + 1) * columns] = jnp.where(
                     own == jnp.asarray(position, BF16), values, jnp.zeros_like(values)
@@ -191,26 +226,6 @@
             device_id_type=MESH,
         )
 
-    index_copy.wait()
-
-    def block_in(to, slot):
-        block = block_of_ref[0, to * slots + slot]
-        return jnp.minimum(jnp.maximum(block, 0), block_count)
-
-    def send_coords(k, carry):
-        to = lax.rem(me_t + k, peers)
-        for slot in range(slots):
-            coords_out[to, slot * BB : (slot + 1) * BB, :] = coord_rows[block_in(to, slot)]
-
-        @pl.when(k < peers)
-        def _():
-            coords_copy(to, me_t, to).start()
-
-        return carry
-
-    lax.fori_loop(1, peers + 1, send_coords, 0)
-    coords_in[me_t] = coords_out[me_t]
-
     def models_copy(group, owner, to):
         return pltpu.make_async_remote_copy(
             src_ref=models_out.at[group],
@@ -221,10 +236,20 @@
             device_id_type=MESH,
         )
 
+    def nth_group(k):
+        far = jnp.where(k < owners // 2, k + owners // 2, owners - 1 - k)
+        return lax.rem(me_d // 2 + far // 2, owners // 2) * 2 + lax.rem(me_d + far, 2)
+
+    def send_coords(k, carry):
+        to = lax.rem(me_t + k, peers)
+        coords_copy(to, me_t, to).start()
+        return carry
+
     def predict_group(k, carry):
-        group = lax.rem(me_d + k, owners)
-        group_coords = coord_rows[pl.ds(group * group_blocks, group_blocks)]
-        group_coords = group_coords.reshape(group_rows, LANES)[:, 0:8]
+        group = nth_group(k)
+        group_coords = coord_rows[
+            pl.ds(pl.multiple_of(group * group_rows, group_rows), group_rows), 0:8
+        ]
         chunks = comps // CHUNK
         buffers = (turned_a, turned_b)
         pieces = group_rows // SUB
@@ -250,8 +275,8 @@
             for sub in range(pieces):
                 rows = slice(sub * SUB, (sub + 1) * SUB)
                 cos_part, sin_part = turn_cos_sin(turns[rows])
-                turned[0, rows, :] = cos_part
-                turned[1, rows, :] = sin_part
+                turned[0, rows, :] = cos_part.astype(BF16)
+                turned[1, rows, :] = sin_part.astype(BF16)
                 if chunk > 0 and sub == 0:
                     update = contract_chunk(chunk - 1, 0)
                 if chunk > 0 and sub == pieces // 2 - 1:
@@ -266,93 +291,121 @@
         last = contract_chunk(chunks - 1, 0) + contract_chunk(chunks - 1, 1)
         final = (acc[...] + last).astype(BF16)
 
-        @pl.when(k < owners)
+        @pl.when(k == 0)
+        def _():
+            pl.semaphore_wait(barrier, owners - 1 + peers - 1)
+
+        @pl.when(k < owners - 1)
         def _():
             models_out[group] = final
             models_copy(group, me_d, group).start()
 
-        @pl.when(k == owners)
+        @pl.when(k == 0)
+        def _():
+            lax.fori_loop(1, peers, send_coords, 0)
+
+        @pl.when(k == owners - 1)
         def _():
             models_in[me_d] = final
 
         return carry
 
-    lax.fori_loop(1, owners + 1, predict_group, 0)
-
-    def wait_coords(k, carry):
-        source = lax.rem(me_t + k, peers)
-        coords_copy(source, source, source).wait()
-        return carry
-
-    lax.fori_loop(1, peers, wait_coords, 0)
-    share = grid_ref.shape[1]
-    pixel = me_d * share + lax.broadcasted_iota(jnp.int32, (share, LANES), 0)
-    which = lax.broadcasted_iota(jnp.int32, (share, LANES), 1)
-    pixel_xy = jnp.where(
-        which == 0,
-        (pixel // GRID - GRID // 2).astype(F32),
-        jnp.where(which == 3, (pixel % GRID - GRID // 2).astype(F32), 0.0),
-    )
-    pixel_xy = (pixel_xy / (2.0 * GRID)).astype(BF16)
-
-    def make_table(source, carry):
-        turns = lax.dot_general(
-            pixel_xy, coords_in[source], (((1,), (1,)), ((), ())), preferred_element_type=F32
-        )
-        cos_part, sin_part = turn_cos_sin(turns)
-        tables[source, 0:share, :] = cos_part
-        tables[source, share : 2 * share, :] = sin_part
-        return carry
-
-    lax.fori_loop(0, peers, make_table, 0)
+    lax.fori_loop(0, owners, predict_group, 0)
+    coords_in[me_t] = coords_out[me_t]
+    index_copy.wait()
+    vis_copy.wait()
 
     def wait_models(k, carry):
-        source = lax.rem(me_d + k, owners)
+        source = nth_group(k)
         models_copy(source, source, source).wait()
         return carry
 
-    lax.fori_loop(1, owners, wait_models, 0)
+    lax.fori_loop(0, owners - 1, wait_models, 0)
 
     gain_blocks = group_rows // GB
-    first = me_d * group_rows
     ridge = jnp.broadcast_to(ridge_ref[...], (8, columns))
     lane = lax.broadcasted_iota(jnp.int32, (8, columns), 1)
-
-    def over_rows(value):
-        total = jnp.sum(jnp.sum(value, axis=0), axis=0, keepdims=True)
-        return jnp.broadcast_to(total, (8, columns))
-
-    def peel_owner(owner, remains):
-        out = []
+    stripe = lax.broadcasted_iota(jnp.int32, (8, columns), 0) // (8 // gain_blocks)
+    reach = 2 * (ITERS - 1)
+
+    def side_by_side(values):
+        total = None
         for block in range(gain_blocks):
-            rest = remains[block]
-            for position in range(DIR_DEV):
-                model = models_in[
+            part = jnp.sum(jnp.sum(values[block], axis=0), axis=0, keepdims=True)
+            part = jnp.broadcast_to(part, (8, columns))
+            total = part if block == 0 else jnp.where(stripe == block, part, total)
+        return total
+
+    def of_block(value, block):
+        row = block * (8 // gain_blocks)
+        return jnp.broadcast_to(value[row : row + 1, :], (8, columns))[None]
+
+    def moved(value, far):
+        rolled = {0: value}
+        for shift in range(2, far + 1, 2):
+            rolled[shift] = pltpu.roll(value, columns - shift, 1)
+            rolled[-shift] = pltpu.roll(value, shift, 1)
+        out = {0: value}
+        for shift in range(2, far + 1, 2):
+            right, left = rolled[shift], rolled[-shift]
+            for step in range(shift // 2):
+                mirror = shift - 2 - 4 * step
+                left = jnp.where(lane // 2 == step, rolled[mirror], left)
+                right = jnp.where(lane // 2 == columns // 2 - 1 - step, rolled[-mirror], right)
+            out[shift], out[-shift] = right, left
+        return out
+
+    def sweep_gain(constant, couple):
+        base = moved(constant, reach)
+        gain = {shift: base[shift] + 2.0 * couple[shift] for shift in base}
+        for sweep in range(1, ITERS):
+            far = reach - 2 * sweep
+            gain = {
+                shift: base[shift] + couple[shift] * (gain[shift - 2] + gain[shift + 2])
+                for shift in range(-far, far + 1, 2)
+            }
+        return gain[0]
+
+    rest = [
+        vis_buf[block * GB : (block + 1) * GB, :].astype(F32).reshape(GB // 8, 8, columns)
+        for block in range(gain_blocks)
+    ]
+
+    def peel_owner(owner, rest):
+        models = [
+            [
+                models_in[
                     owner,
                     block * GB : (block + 1) * GB,
                     position * columns : (position + 1) * columns,
-                ].astype(F32)
-                model = model.reshape(GB // 8, 8, columns)
-                cross_sum = over_rows(rest * model)
-                inverse = 1.0 / (over_rows(model * model) + ridge)
-                gain = jnp.ones_like(cross_sum)
-                for sweep in range(ITERS):
-                    before = jnp.where(lane < 2, gain, pltpu.roll(gain, 2, 1))
-                    after = jnp.where(
-                        lane >= columns - 2, gain, pltpu.roll(gain, columns - 2, 1)
-                    )
-                    gain = (cross_sum + ridge * (0.5 * (before + after))) * inverse
-                rest = rest - gain[None] * model
-            out.append(rest.astype(BF16).astype(F32))
+                ]
+                .astype(F32)
+                .reshape(GB // 8, 8, columns)
+                for block in range(gain_blocks)
+            ]
+            for position in range(DIR_DEV)
+        ]
+        every = range(gain_blocks)
+        gains = []
+        for position in range(DIR_DEV):
+            model = models[position]
+            inverse = 1.0 / (side_by_side([model[b] * model[b] for b in every]) + ridge)
+            couple = moved(0.5 * ridge * inverse, reach)
+            cross_sum = side_by_side([rest[b] * model[b] for b in every])
+            for earlier_one in range(position):
+                other = models[earlier_one]
+                shared = side_by_side([other[b] * model[b] for b in every])
+                cross_sum = cross_sum - gains[earlier_one] * shared
+            gains.append(sweep_gain(cross_sum * inverse, couple))
+        out = []
+        for b in every:
+            left = rest[b]
+            for position in range(DIR_DEV):
+                left = left - of_block(gains[position], b) * models[position][b]
+            out.append(left.astype(BF16).astype(F32))
         return tuple(out)
 
-    start = tuple(
-        vis_ref[pl.ds(pl.multiple_of(first + block * GB, GB), GB), :]
-        .astype(F32)
-        .reshape(GB // 8, 8, columns)
-        for block in range(gain_blocks)
-    )
-    done = lax.fori_loop(0, owners, peel_owner, start)
+    done = lax.fori_loop(0, owners, peel_owner, tuple(rest))
     per_gain = GB // BB
     for block in range(gain_blocks):
         resid[pl.ds(me_d * group_blocks + block * per_gain, per_gain)] = (
@@ -378,37 +431,117 @@
         source = lax.rem(me_d + k, owners)
         resid_copy(source, source, source).wait_recv()
 
+    def block_in(to, slot):
+        block = block_of_ref[0, to * slots + slot]
+        return jnp.minimum(jnp.maximum(block, 0), block_count)
+
+    def half_of(which):
+        return pl.ds(pl.multiple_of(which * half_rows, half_rows), half_rows)
+
     def rows_copy(src, owner, to):
         return pltpu.make_async_remote_copy(
             src_ref=rows_out.at[src],
-            dst_ref=rows_in.at[owner],
+            dst_ref=rows_in.at[owner, half_of(core)],
             send_sem=d_send.at[src],
             recv_sem=d_recv.at[owner],
             device_id={"tb": to},
             device_id_type=MESH,
         )
 
+    def hand_over(owner, which):
+        return pltpu.make_async_remote_copy(
+            src_ref=rows_in.at[owner, half_of(which)],
+            dst_ref=rows_in.at[owner, half_of(which)],
+            send_sem=f_send.at[owner],
+            recv_sem=f_recv.at[owner],
+            device_id={"dir": partner},
+            device_id_type=MESH,
+        )
+
     def dispatch(k, carry):
         to = lax.rem(me_t + k, peers)
-        for slot in range(slots):
-            rows_out[to, slot * BB : (slot + 1) * BB, :] = resid[block_in(to, slot)]
-
-        @pl.when(k < peers)
+        for slot in range(half_slots):
+            rows_out[to, slot * BB : (slot + 1) * BB, :] = resid[
+                block_in(to, core * half_slots + slot)
+            ]
+        rows_copy(to, me_t, to).start()
+        return carry
+
+    lax.fori_loop(1, peers, dispatch, 0)
+    for slot in range(slots):
+        own_rows[slot * BB : (slot + 1) * BB, :] = resid[block_in(me_t, slot)]
+    resid_ref[...] = resid[0:block_count].reshape(sample_rows, columns)
+
+    def wait_coords(k, carry):
+        source = lax.rem(me_t + k, peers)
+        coords_copy(source, source, source).wait()
+        return carry
+
+    lax.fori_loop(1, peers, wait_coords, 0)
+    share = grid_ref.shape[1]
+    lines = share // GRID
+    slots_wide = LANES // BB
+    strips_wide = -(-slot_rows // LANES)
+    wide = strips_wide * LANES
+    x_of = (
+        me_d * lines - GRID // 2 + lax.broadcasted_iota(jnp.int32, (lines, wide), 0)
+    ).astype(F32) / (2.0 * GRID)
+    y_of = (lax.broadcasted_iota(jnp.int32, (GRID, wide), 0) - GRID // 2).astype(F32) / (
+        2.0 * GRID
+    )
+    slot_at = lax.broadcasted_iota(jnp.int32, (side, LANES), 0)
+    slot_for = lax.broadcasted_iota(jnp.int32, (side, LANES), 1) // BB
+
+    def make_table(source, carry):
+        given = coords_in[source].astype(F32)
+
+        def flat(rows):
+            return jnp.concatenate(
+                [
+                    jnp.sum(
+                        jnp.where(slot_at == slot_for + strip * slots_wide, rows, 0.0),
+                        axis=0,
+                        keepdims=True,
+                    )
+                    for strip in range(strips_wide)
+                ],
+                axis=1,
+            )
+
+        cos_x, sin_x = turn_cos_sin(x_of * flat(given[0:side]))
+        cos_y, sin_y = turn_cos_sin(y_of * flat(given[side:packed]))
+        for line in range(lines):
+            cos_l, sin_l = cos_x[line : line + 1], sin_x[line : line + 1]
+            rows = slice(line * GRID, (line + 1) * GRID)
+            lower = slice(share + line * GRID, share + (line + 1) * GRID)
+            cos_part = (cos_l * cos_y - sin_l * sin_y).astype(BF16)
+            sin_part = (sin_l * cos_y + cos_l * sin_y).astype(BF16)
+            tables[source, rows, :] = cos_part[:, 0:slot_rows]
+            tables[source, lower, :] = sin_part[:, 0:slot_rows]
+        return carry
+
+    lax.fori_loop(0, peers, make_table, 0)
+
+    grid_sum = jnp.dot(tables[me_t], own_rows[...], preferred_element_type=F32)
+
+    def source_at(k):
+        return lax.rem(me_t + peers - k, peers)
+
+    def arrive(k):
+        source = source_at(k)
+        rows_copy(source, source, source).wait_recv()
+        hand_over(source, core).start()
+
+    def add_source(k, total):
+        @pl.when(k + 1 < peers)
         def _():
-            rows_copy(to, me_t, to).start()
-
-        return carry
-
-    lax.fori_loop(1, peers + 1, dispatch, 0)
-    resid_ref[...] = resid[0:block_count].reshape(sample_rows, columns)
-
-    grid_sum = jnp.dot(tables[me_t], rows_out[me_t], preferred_element_type=F32)
-
-    def add_source(k, total):
-        source = lax.rem(me_t + k, peers)
-        rows_copy(source, source, source).wait_recv()
+            arrive(k + 1)
+
+        source = source_at(k)
+        hand_over(source, 1 - core).wait_recv()
         return total + jnp.dot(tables[source], rows_in[source], preferred_element_type=F32)
 
+    arrive(1)
     grid_sum = lax.fori_loop(1, peers, add_source, grid_sum)
     grid_ref[...] = (grid_sum * float(ROWS_DEV) ** (-0.5)).reshape(2, share, columns)
 
@@ -419,6 +552,7 @@
     def drain(k, carry):
         to = lax.rem(me_t + k, peers)
         rows_copy(to, me_t, to).wait_send()
+        hand_over(to, core).wait_send()
         return carry
 
     lax.fori_loop(1, peers, drain, 0)
@@ -454,8 +588,12 @@
     share = PIX // owners
 
     slot_lanes = -(-peers * slots // LANES) * LANES
+    packed = 16 * -(-slots // 8)
+    group_rows = sample_rows // owners
+    half_rows = slots // 2 * BB
     vmem = pl.BlockSpec(memory_space=pltpu.VMEM)
     smem = pl.BlockSpec(memory_space=pltpu.SMEM)
+    anywhere = pl.BlockSpec(memory_space=pl.ANY)
     dma = pltpu.SemaphoreType.DMA
     residual, subgrid = pl.pallas_call(
         functools.partial(kernel, owners, peers, slots),
@@ -463,24 +601,27 @@
             jax.ShapeDtypeStruct((sample_rows, columns), BF16),
             jax.ShapeDtypeStruct((2, share, columns), F32),
         ),
-        in_specs=[vmem] * 7 + [smem],
+        in_specs=[vmem] * 5 + [smem] + [anywhere] * 2,
         out_specs=(vmem, vmem),
         scratch_shapes=[
+            pltpu.VMEM((group_rows, columns), BF16),
+            pltpu.VMEM((2, comps, columns), BF16),
             pltpu.VMEM((2, comps, DIR_DEV * columns), BF16),
             pltpu.VMEM((8, comps), BF16),
-            pltpu.VMEM((block_count + 1, BB, LANES), BF16),
+            pltpu.VMEM((sample_rows, LANES), BF16),
             pltpu.VMEM((1, slot_lanes), jnp.int32),
             pltpu.SMEM((1, slot_lanes), jnp.int32),
-            pltpu.VMEM((peers, slots * BB, LANES), BF16),
-            pltpu.VMEM((2, sample_rows // owners, CHUNK), BF16),
-            pltpu.VMEM((2, sample_rows // owners, CHUNK), BF16),
-            pltpu.VMEM((sample_rows // owners, DIR_DEV * columns), F32),
-            pltpu.VMEM((owners, sample_rows // owners, DIR_DEV * columns), BF16),
-            pltpu.VMEM((owners, sample_rows // owners, DIR_DEV * columns), BF16),
+            pltpu.VMEM((peers, packed, LANES), BF16),
+            pltpu.VMEM((2, group_rows, CHUNK), BF16),
+            pltpu.VMEM((2, group_rows, CHUNK), BF16),
+            pltpu.VMEM((group_rows, DIR_DEV * columns), F32),
+            pltpu.VMEM((owners, group_rows, DIR_DEV * columns), BF16),
+            pltpu.VMEM((owners, group_rows, DIR_DEV * columns), BF16),
             pltpu.VMEM((block_count + 1, BB, columns), BF16),
+            pltpu.VMEM((slots * BB, columns), BF16),
+            pltpu.VMEM((peers, half_rows, columns), BF16),
             pltpu.VMEM((peers, slots * BB, columns), BF16),
-            pltpu.VMEM((peers, slots * BB, columns), BF16),
-            pltpu.VMEM((peers, slots * BB, LANES), BF16),
+            pltpu.VMEM((peers, packed, LANES), BF16),
             pltpu.VMEM((peers, 2 * share, slots * BB), BF16),
             dma((owners,)),
             dma((owners,)),
@@ -490,22 +631,23 @@
             dma((peers,)),
             dma((peers,)),
             dma((peers,)),
-            dma,
+            dma((peers,)),
+            dma((peers,)),
+            dma((3,)),
         ],
         compiler_params=pltpu.CompilerParams(
             collective_id=0, has_side_effects=True, vmem_limit_bytes=60 * 1024 * 1024
         ),
     )(
-        visibilities,
         uv_coords,
         comp_lm,
-        spectra,
         ridge_weight[None, :],
         assignment.reshape(comps // LANES, LANES),
         block_tile.reshape(1, block_count),
         peel_order,
-    )
-    anywhere = pl.BlockSpec(memory_space=pl.ANY)
+        visibilities,
+        spectra,
+    )
     residual, subgrid = pl.pallas_call(
         finish,
         out_shape=(

time: 49.2 us -> 39.1 us (0.79)
  the two profiles are of different devices: /device:TPU:13 before, /device:TPU:0 now
where the time goes in v1:
time: 39.1 us; the launch traced here: 38.8 us
  Pallas kernels  38.2 us (98%)
  between operations  0.64 us (2%)
    pallas_call x1, Pallas kernels, local(): pl.pallas_call(functools.partial(kernel, owners, peers, slots), out_shape...  36.4 us
    pallas_call x1, Pallas kernels, local(): pl.pallas_call(finish, out_shape=(jax.ShapeDtypeStruct(residual.shape, re...  1.83 us

profile of v1, /device:TPU:0, one launch (start us, length us, event | category | flops | bytes accessed | tf_op | source)
XLA Modules:
  0.0 38.8 jit_solution(10510586624890670070)
XLA Ops:
  0.6 36.4 %shard_map.95 = (bf16[1024,128]{1,0:T(8,128)(2,1)}, f32[2,256,128]{2,1,0:T(8,128)}) custom-call(bf16[2,1024]{1,0:T(2,128)(2,1)} %uv_ref.1, f32[2,3072]{1,0:T(2,128)} %lm_ref.1, f32[1,128]{1,0:T(1,128)} %bitcast.5, s32[24,128]{1,0:T(8,128)} %bitcast.4, s32[1,32]{1,0:T(1,128)} %bitcast.6, s32[3]{0:T(128)} %peel_ref.1, bf16[1024,128]{1,0:T(8,128)(2,1)} %vis_hbm.1, ...), custom_call_target="tpu_custom_call" | custom-call | tf_op jit(solution)/shard_map/pallas_call | solution.py:598
  37.0 1.8 %shard_map.96 = (bf16[1024,128]{1,0:T(8,128)(2,1)}, f32[2,256,128]{2,1,0:T(8,128)}) custom-call(bf16[1024,128]{1,0:T(8,128)(2,1)} %get-tuple-element.6.resid_ref, f32[2,256,128]{2,1,0:T(8,128)} %get-tuple-element.7.grid_ref), custom_call_target="tpu_custom_call" | custom-call | tf_op jit(solution)/shard_map/pallas_call | solution.py:651

commit v2 on v1

--- a/solution.py
+++ b/solution.py
@@ -28,10 +28,14 @@
 COS_FIT = (1.414204014809076, -6.977637323456295, 5.715187874756718, -1.728213892223522)
 
 
+BENT_SIN = (6.28125, -41.25, 76.5)
+BENT_COS = (1.0, -19.75, 65.0, -79.5)
+
+
 def horner(square, fit):
-    total = fit[-1]
+    total = jnp.asarray(fit[-1], square.dtype)
     for coefficient in fit[-2::-1]:
-        total = total * square + coefficient
+        total = total * square + jnp.asarray(coefficient, square.dtype)
     return total
 
 
@@ -41,6 +45,15 @@
     half_sin = part * horner(square, SIN_FIT)
     half_cos = horner(square, COS_FIT)
     return 1.0 - half_sin * half_sin, half_sin * half_cos
+
+
+def turn_cos_sin_short(turns):
+    part = turns - jnp.round(turns)
+    bent = (0.25 - jnp.abs(part)).astype(BF16)
+    square = bent * bent
+    upright = horner(square, BENT_COS)
+    flipped = jnp.where(part.astype(BF16) < 0, -upright, upright)
+    return bent * horner(square, BENT_SIN), flipped
 
 
 def kernel(
@@ -174,7 +187,7 @@
     coords_out[...] = sent.astype(BF16).reshape(peers, packed, LANES)
 
     stacked = jnp.concatenate(
-        [u_row] * 3 + [v_row] * 3 + [jnp.zeros((LANES - 6, sample_rows), F32)], axis=0
+        [u_row] * 3 + [v_row] * 3 + [jnp.zeros((2, sample_rows), F32)], axis=0
     )
     coord_rows[...] = stacked.T.astype(BF16)
 
@@ -226,33 +239,46 @@
             device_id_type=MESH,
         )
 
-    def models_copy(group, owner, to):
+    gain_blocks = group_rows // GB
+    pairs = owners // 2
+
+    def models_copy(group, owner, part, to):
+        rows = pl.ds(pl.multiple_of(part * GB, GB), GB)
         return pltpu.make_async_remote_copy(
-            src_ref=models_out.at[group],
-            dst_ref=models_in.at[owner],
-            send_sem=m_send.at[group],
-            recv_sem=m_recv.at[owner],
+            src_ref=models_out.at[group, rows],
+            dst_ref=models_in.at[owner, rows],
+            send_sem=m_send.at[part, group],
+            recv_sem=m_recv.at[part, owner],
             device_id={"dir": to},
             device_id_type=MESH,
         )
-
-    def nth_group(k):
-        far = jnp.where(k < owners // 2, k + owners // 2, owners - 1 - k)
-        return lax.rem(me_d // 2 + far // 2, owners // 2) * 2 + lax.rem(me_d + far, 2)
 
     def send_coords(k, carry):
         to = lax.rem(me_t + k, peers)
         coords_copy(to, me_t, to).start()
         return carry
 
-    def predict_group(k, carry):
-        group = nth_group(k)
-        group_coords = coord_rows[
-            pl.ds(pl.multiple_of(group * group_rows, group_rows), group_rows), 0:8
-        ]
+    def predict_step(step, carry):
+        part = lax.rem(step, gain_blocks)
+        nearness = step // gain_blocks
+        chip = lax.rem(me_d // 2 + 1 + nearness, pairs)
+        span = pl.ds(pl.multiple_of(part * GB, GB), GB)
+        group_coords = jnp.concatenate(
+            [
+                coord_rows[
+                    pl.ds(
+                        pl.multiple_of((2 * chip + side_of) * group_rows + part * GB, GB), GB
+                    ),
+                    :,
+                ]
+                for side_of in range(2)
+            ],
+            axis=0,
+        )
+        step_rows = 2 * GB
         chunks = comps // CHUNK
         buffers = (turned_a, turned_b)
-        pieces = group_rows // SUB
+        pieces = step_rows // SUB
 
         def spread_turns(chunk):
             return jnp.dot(
@@ -274,9 +300,9 @@
             following = None
             for sub in range(pieces):
                 rows = slice(sub * SUB, (sub + 1) * SUB)
-                cos_part, sin_part = turn_cos_sin(turns[rows])
-                turned[0, rows, :] = cos_part.astype(BF16)
-                turned[1, rows, :] = sin_part.astype(BF16)
+                cos_part, sin_part = turn_cos_sin_short(turns[rows])
+                turned[0, rows, :] = cos_part
+                turned[1, rows, :] = sin_part
                 if chunk > 0 and sub == 0:
                     update = contract_chunk(chunk - 1, 0)
                 if chunk > 0 and sub == pieces // 2 - 1:
@@ -291,54 +317,41 @@
         last = contract_chunk(chunks - 1, 0) + contract_chunk(chunks - 1, 1)
         final = (acc[...] + last).astype(BF16)
 
-        @pl.when(k == 0)
+        @pl.when(step == 0)
         def _():
             pl.semaphore_wait(barrier, owners - 1 + peers - 1)
 
-        @pl.when(k < owners - 1)
-        def _():
-            models_out[group] = final
-            models_copy(group, me_d, group).start()
-
-        @pl.when(k == 0)
+        for side_of in range(2):
+            group = 2 * chip + side_of
+            piece = final[side_of * GB : (side_of + 1) * GB]
+
+            @pl.when(group != me_d)
+            def _():
+                models_out[group, span, :] = piece
+                models_copy(group, me_d, part, group).start()
+
+            @pl.when(group == me_d)
+            def _():
+                models_in[me_d, span, :] = piece
+
+        @pl.when(step == 0)
         def _():
             lax.fori_loop(1, peers, send_coords, 0)
 
-        @pl.when(k == owners - 1)
-        def _():
-            models_in[me_d] = final
-
         return carry
 
-    lax.fori_loop(0, owners, predict_group, 0)
+    lax.fori_loop(0, pairs * gain_blocks, predict_step, 0)
     coords_in[me_t] = coords_out[me_t]
     index_copy.wait()
     vis_copy.wait()
 
-    def wait_models(k, carry):
-        source = nth_group(k)
-        models_copy(source, source, source).wait()
-        return carry
-
-    lax.fori_loop(0, owners - 1, wait_models, 0)
-
-    gain_blocks = group_rows // GB
     ridge = jnp.broadcast_to(ridge_ref[...], (8, columns))
     lane = lax.broadcasted_iota(jnp.int32, (8, columns), 1)
-    stripe = lax.broadcasted_iota(jnp.int32, (8, columns), 0) // (8 // gain_blocks)
     reach = 2 * (ITERS - 1)
 
-    def side_by_side(values):
-        total = None
-        for block in range(gain_blocks):
-            part = jnp.sum(jnp.sum(values[block], axis=0), axis=0, keepdims=True)
-            part = jnp.broadcast_to(part, (8, columns))
-            total = part if block == 0 else jnp.where(stripe == block, part, total)
-        return total
-
-    def of_block(value, block):
-        row = block * (8 // gain_blocks)
-        return jnp.broadcast_to(value[row : row + 1, :], (8, columns))[None]
+    def over_rows(value):
+        total = jnp.sum(jnp.sum(value, axis=0), axis=0, keepdims=True)
+        return jnp.broadcast_to(total, (8, columns))
 
     def moved(value, far):
         rolled = {0: value}
@@ -366,70 +379,63 @@
             }
         return gain[0]
 
-    rest = [
-        vis_buf[block * GB : (block + 1) * GB, :].astype(F32).reshape(GB // 8, 8, columns)
-        for block in range(gain_blocks)
-    ]
-
-    def peel_owner(owner, rest):
+    per_gain = GB // BB
+
+    def peel_owner(part, owner, rest):
         models = [
-            [
-                models_in[
-                    owner,
-                    block * GB : (block + 1) * GB,
-                    position * columns : (position + 1) * columns,
-                ]
-                .astype(F32)
-                .reshape(GB // 8, 8, columns)
-                for block in range(gain_blocks)
+            models_in[
+                owner,
+                part * GB : (part + 1) * GB,
+                position * columns : (position + 1) * columns,
             ]
+            .astype(F32)
+            .reshape(GB // 8, 8, columns)
             for position in range(DIR_DEV)
         ]
-        every = range(gain_blocks)
         gains = []
         for position in range(DIR_DEV):
             model = models[position]
-            inverse = 1.0 / (side_by_side([model[b] * model[b] for b in every]) + ridge)
+            inverse = 1.0 / (over_rows(model * model) + ridge)
             couple = moved(0.5 * ridge * inverse, reach)
-            cross_sum = side_by_side([rest[b] * model[b] for b in every])
-            for earlier_one in range(position):
-                other = models[earlier_one]
-                shared = side_by_side([other[b] * model[b] for b in every])
-                cross_sum = cross_sum - gains[earlier_one] * shared
+            cross_sum = over_rows(rest * model)
+            for before in range(position):
+                cross_sum = cross_sum - gains[before] * over_rows(models[before] * model)
             gains.append(sweep_gain(cross_sum * inverse, couple))
-        out = []
-        for b in every:
-            left = rest[b]
-            for position in range(DIR_DEV):
-                left = left - of_block(gains[position], b) * models[position][b]
-            out.append(left.astype(BF16).astype(F32))
-        return tuple(out)
-
-    done = lax.fori_loop(0, owners, peel_owner, tuple(rest))
-    per_gain = GB // BB
-    for block in range(gain_blocks):
-        resid[pl.ds(me_d * group_blocks + block * per_gain, per_gain)] = (
-            done[block].reshape(per_gain, BB, columns).astype(BF16)
-        )
-    resid[block_count] = jnp.zeros((BB, columns), BF16)
-
-    def resid_copy(group, sem, to):
-        part = pl.ds(group * group_blocks, group_blocks)
+        for position in range(DIR_DEV):
+            rest = rest - gains[position][None] * models[position]
+        return rest.astype(BF16).astype(F32)
+
+    def resid_copy(group, part, sem, to):
+        span = pl.ds(group * group_blocks + part * per_gain, per_gain)
         return pltpu.make_async_remote_copy(
-            src_ref=resid.at[part],
-            dst_ref=resid.at[part],
-            send_sem=r_send.at[sem],
-            recv_sem=r_recv.at[group],
+            src_ref=resid.at[span],
+            dst_ref=resid.at[span],
+            send_sem=r_send.at[part, sem],
+            recv_sem=r_recv.at[part, group],
             device_id={"dir": to},
             device_id_type=MESH,
         )
 
-    for k in range(1, owners):
-        to = lax.rem(me_d + k, owners)
-        resid_copy(me_d, to, to).start()
-    for k in range(1, owners):
-        source = lax.rem(me_d + k, owners)
-        resid_copy(source, source, source).wait_recv()
+    for part in range(gain_blocks):
+        for k in range(1, owners):
+            source = lax.rem(me_d + k, owners)
+            models_copy(source, source, part, source).wait()
+        rest = (
+            vis_buf[part * GB : (part + 1) * GB, :].astype(F32).reshape(GB // 8, 8, columns)
+        )
+        for owner in range(owners):
+            rest = peel_owner(part, owner, rest)
+        resid[pl.ds(me_d * group_blocks + part * per_gain, per_gain)] = rest.reshape(
+            per_gain, BB, columns
+        ).astype(BF16)
+        for k in range(1, owners):
+            to = lax.rem(me_d + k, owners)
+            resid_copy(me_d, part, to, to).start()
+    resid[block_count] = jnp.zeros((BB, columns), BF16)
+    for part in range(gain_blocks):
+        for k in range(1, owners):
+            source = lax.rem(me_d + k, owners)
+            resid_copy(source, part, source, source).wait_recv()
 
     def block_in(to, slot):
         block = block_of_ref[0, to * slots + slot]
@@ -545,9 +551,10 @@
     grid_sum = lax.fori_loop(1, peers, add_source, grid_sum)
     grid_ref[...] = (grid_sum * float(ROWS_DEV) ** (-0.5)).reshape(2, share, columns)
 
-    for k in range(1, owners):
-        to = lax.rem(me_d + k, owners)
-        resid_copy(me_d, to, to).wait_send()
+    for part in range(gain_blocks):
+        for k in range(1, owners):
+            to = lax.rem(me_d + k, owners)
+            resid_copy(me_d, part, to, to).wait_send()
 
     def drain(k, carry):
         to = lax.rem(me_t + k, peers)
@@ -598,8 +605,8 @@
     residual, subgrid = pl.pallas_call(
         functools.partial(kernel, owners, peers, slots),
         out_shape=(
-            jax.ShapeDtypeStruct((sample_rows, columns), BF16),
-            jax.ShapeDtypeStruct((2, share, columns), F32),
+            pltpu.VMEM((sample_rows, columns), BF16),
+            pltpu.VMEM((2, share, columns), F32),
         ),
         in_specs=[vmem] * 5 + [smem] + [anywhere] * 2,
         out_specs=(vmem, vmem),
@@ -608,13 +615,13 @@
             pltpu.VMEM((2, comps, columns), BF16),
             pltpu.VMEM((2, comps, DIR_DEV * columns), BF16),
             pltpu.VMEM((8, comps), BF16),
-            pltpu.VMEM((sample_rows, LANES), BF16),
+            pltpu.VMEM((sample_rows, 8), BF16),
             pltpu.VMEM((1, slot_lanes), jnp.int32),
             pltpu.SMEM((1, slot_lanes), jnp.int32),
             pltpu.VMEM((peers, packed, LANES), BF16),
-            pltpu.VMEM((2, group_rows, CHUNK), BF16),
-            pltpu.VMEM((2, group_rows, CHUNK), BF16),
-            pltpu.VMEM((group_rows, DIR_DEV * columns), F32),
+            pltpu.VMEM((2, 2 * GB, CHUNK), BF16),
+            pltpu.VMEM((2, 2 * GB, CHUNK), BF16),
+            pltpu.VMEM((2 * GB, DIR_DEV * columns), F32),
             pltpu.VMEM((owners, group_rows, DIR_DEV * columns), BF16),
             pltpu.VMEM((owners, group_rows, DIR_DEV * columns), BF16),
             pltpu.VMEM((block_count + 1, BB, columns), BF16),
@@ -623,10 +630,10 @@
             pltpu.VMEM((peers, slots * BB, columns), BF16),
             pltpu.VMEM((peers, packed, LANES), BF16),
             pltpu.VMEM((peers, 2 * share, slots * BB), BF16),
-            dma((owners,)),
-            dma((owners,)),
-            dma((owners,)),
-            dma((owners,)),
+            dma((group_rows // GB, owners)),
+            dma((group_rows // GB, owners)),
+            dma((group_rows // GB, owners)),
+            dma((group_rows // GB, owners)),
             dma((peers,)),
             dma((peers,)),
             dma((peers,)),
@@ -657,7 +664,10 @@
         in_specs=[vmem] * 2,
         out_specs=(anywhere, anywhere),
         scratch_shapes=[dma((2,))],
-    )(residual, subgrid)
+    )(
+        pltpu.with_memory_space_constraint(residual, pltpu.VMEM),
+        pltpu.with_memory_space_constraint(subgrid, pltpu.VMEM),
+    )
     return residual, subgrid[None]
 
 

time: 39.1 us -> 34.8 us (0.89)
  Pallas kernels: 38.2 us -> 33.9 us
    pallas_call x1, Pallas kernels: 36.4 us -> 33.1 us  [local(): pl.pallas_call(functools.partial(kernel, owners, peers, slots), out_shape...]
    pallas_call x1, Pallas kernels: 1.83 us -> 0.81 us  [local(): pl.pallas_call(finish, out_shape=(jax.ShapeDtypeStruct(residual.shape, re...]
where the time goes in v2:
time: 34.8 us; the launch traced here: 34.5 us
  Pallas kernels  33.9 us (97%)
  between operations  0.64 us (2%)
    pallas_call x1, Pallas kernels, local(): pl.pallas_call(functools.partial(kernel, owners, peers, slots), out_shape...  33.1 us
    pallas_call x1, Pallas kernels, local(): pl.pallas_call(finish, out_shape=(jax.ShapeDtypeStruct(residual.shape, re...  0.81 us

profile of v2, /device:TPU:0, one launch (start us, length us, event | category | flops | bytes accessed | tf_op | source)
XLA Modules:
  0.0 34.5 jit_solution(6408979240991288154)
XLA Ops:
  0.6 33.1 %shard_map.95 = (bf16[1024,128]{1,0:T(8,128)(2,1)S(1)}, f32[2,256,128]{2,1,0:T(8,128)S(1)}) custom-call(bf16[2,1024]{1,0:T(2,128)(2,1)} %uv_ref.1, f32[2,3072]{1,0:T(2,128)} %lm_ref.1, f32[1,128]{1,0:T(1,128)} %bitcast.5, s32[24,128]{1,0:T(8,128)} %bitcast.4, s32[1,32]{1,0:T(1,128)} %bitcast.6, s32[3]{0:T(128)} %peel_ref.1, bf16[1024,128]{1,0:T(8,128)(2,1)} %vis_hbm.1, ...), custom_call_target="tpu_custom_call" | custom-call | tf_op jit(solution)/shard_map/pallas_call | solution.py:605
  33.7 0.8 %shard_map.96 = (bf16[1024,128]{1,0:T(8,128)(2,1)}, f32[2,256,128]{2,1,0:T(8,128)}) custom-call(bf16[1024,128]{1,0:T(8,128)(2,1)S(1)} %get-tuple-element.6.resid_ref, f32[2,256,128]{2,1,0:T(8,128)S(1)} %get-tuple-element.7.grid_ref), custom_call_target="tpu_custom_call" | custom-call | tf_op jit(solution)/shard_map/pallas_call | solution.py:658

commit v3 on v2

--- a/solution.py
+++ b/solution.py
@@ -60,18 +60,24 @@
     owners,
     peers,
     slots,
-    uv_ref,
-    lm_ref,
-    ridge_ref,
-    entry_ref,
-    tile_ref,
-    peel_ref,
+    lm_hbm,
+    entry_hbm,
+    peel_hbm,
+    uv_hbm,
+    spec_hbm,
     vis_hbm,
-    spec_hbm,
+    ridge_hbm,
+    tile_hbm,
     resid_ref,
     grid_ref,
+    lm_ref,
+    entry_ref,
+    peel_ref,
+    uv_ref,
+    spec_buf,
     vis_buf,
-    spec_buf,
+    ridge_ref,
+    tile_ref,
     masked,
     lm_parts,
     coord_rows,
@@ -115,12 +121,24 @@
     half_rows = half_slots * BB
     first = me_d * group_rows
 
-    spec_copy = pltpu.make_async_copy(spec_hbm, spec_buf, local_sem.at[0])
-    vis_copy = pltpu.make_async_copy(
-        vis_hbm.at[pl.ds(pl.multiple_of(first, group_rows), group_rows)], vis_buf, local_sem.at[1]
-    )
-    spec_copy.start()
-    vis_copy.start()
+    own_part = vis_hbm.at[pl.ds(pl.multiple_of(first, group_rows), group_rows)]
+    fetches = [
+        pltpu.make_async_copy(source, target, local_sem.at[number])
+        for number, (source, target) in enumerate(
+            (
+                (lm_hbm, lm_ref),
+                (entry_hbm, entry_ref),
+                (peel_hbm, peel_ref),
+                (uv_hbm, uv_ref),
+                (spec_hbm, spec_buf),
+                (own_part, vis_buf),
+                (ridge_hbm, ridge_ref),
+                (tile_hbm, tile_ref),
+            )
+        )
+    ]
+    for fetch in fetches:
+        fetch.start()
 
     barrier = pltpu.get_barrier_semaphore()
     for k in range(1, owners):
@@ -136,56 +154,11 @@
 
     lax.fori_loop(1, peers, greet, 0)
 
-    slot_lanes = block_row.shape[1]
-    tiles = jnp.broadcast_to(tile_ref[...], (slot_lanes, block_count))
-    named_tile = jnp.where(
-        lax.broadcasted_iota(jnp.int32, (slot_lanes, block_count), 0) == tiles, 1.0, 0.0
-    )
-    earlier = jnp.where(
-        lax.broadcasted_iota(jnp.int32, (block_count, block_count), 0)
-        < lax.broadcasted_iota(jnp.int32, (block_count, block_count), 1),
-        1.0,
-        0.0,
-    )
-    ranks = jnp.dot(named_tile.astype(BF16), earlier.astype(BF16), preferred_element_type=F32)
-    slot = jnp.sum(ranks * named_tile, axis=0, keepdims=True).astype(jnp.int32)
-    target = jnp.broadcast_to(tile_ref[...] * slots + slot, (slot_lanes, block_count))
-    lane = lax.broadcasted_iota(jnp.int32, (slot_lanes, block_count), 0)
-    taken = jnp.where(lane == target, 1.0, 0.0).astype(BF16)
-    block_id = lax.broadcasted_iota(jnp.int32, (8, block_count), 1) - block_count
-    picked = lax.dot_general(
-        block_id.astype(F32).astype(BF16),
-        taken,
-        (((1,), (1,)), ((), ())),
-        preferred_element_type=F32,
-    )
-    block_row[...] = picked[0:1, :].astype(jnp.int32) + block_count
-    index_copy = pltpu.make_async_copy(block_row, block_of_ref, local_sem.at[2])
-    index_copy.start()
+    for fetch in fetches[0:4]:
+        fetch.wait()
 
     u_row = uv_ref[0:1, :].astype(F32)
     v_row = uv_ref[1:2, :].astype(F32)
-    in_block = (
-        lax.broadcasted_iota(jnp.int32, (block_count, sample_rows), 1) // BB
-        == lax.broadcasted_iota(jnp.int32, (block_count, sample_rows), 0)
-    )
-    at_lane = jnp.where(
-        lax.broadcasted_iota(jnp.int32, (sample_rows, LANES), 0) % BB
-        == lax.broadcasted_iota(jnp.int32, (sample_rows, LANES), 1) % BB,
-        1.0,
-        0.0,
-    ).astype(BF16)
-    packed, side = coords_out.shape[1], coords_out.shape[1] // 2
-    spot = lax.broadcasted_iota(jnp.int32, (peers * packed, block_count), 0)
-    place_of = tile_ref[...] * packed + slot
-    sent = jnp.zeros((peers * packed, LANES), F32)
-    for which, row in enumerate((u_row, v_row)):
-        spread = jnp.where(in_block, jnp.broadcast_to(row, in_block.shape), 0.0).astype(BF16)
-        by_block = jnp.dot(spread, at_lane, preferred_element_type=F32).astype(BF16)
-        chosen = jnp.where(spot == place_of + which * side, 1.0, 0.0).astype(BF16)
-        sent = sent + jnp.dot(chosen, by_block, preferred_element_type=F32)
-    coords_out[...] = sent.astype(BF16).reshape(peers, packed, LANES)
-
     stacked = jnp.concatenate(
         [u_row] * 3 + [v_row] * 3 + [jnp.zeros((2, sample_rows), F32)], axis=0
     )
@@ -218,14 +191,16 @@
     positions = lax.dot_general(
         at_low, at_high, (((1,), (1,)), ((), ())), preferred_element_type=F32
     )
-    spec_copy.wait()
+    fetches[4].wait()
     for strip in range(strips):
         own = jnp.broadcast_to(positions[:, strip : strip + 1], (LANES, columns)).astype(BF16)
         span = pl.ds(strip * LANES, LANES)
+        chunk, inside = strip * LANES // CHUNK, strip * LANES % CHUNK
         for part in range(2):
             values = spec_buf[part, span, :]
+            target_span = pl.ds((2 * chunk + part) * CHUNK + inside, LANES)
             for position in range(DIR_DEV):
-                masked[part, span, position * columns : (position + 1) * columns] = jnp.where(
+                masked[target_span, position * columns : (position + 1) * columns] = jnp.where(
                     own == jnp.asarray(position, BF16), values, jnp.zeros_like(values)
                 )
 
@@ -287,10 +262,10 @@
                 preferred_element_type=F32,
             )
 
-        def contract_chunk(chunk, part):
+        def contract_chunk(chunk):
             return jnp.dot(
-                buffers[chunk % 2][part],
-                masked[part, chunk * CHUNK : (chunk + 1) * CHUNK, :],
+                buffers[chunk % 2][...],
+                masked[2 * chunk * CHUNK : 2 * (chunk + 1) * CHUNK, :],
                 preferred_element_type=F32,
             )
 
@@ -301,12 +276,10 @@
             for sub in range(pieces):
                 rows = slice(sub * SUB, (sub + 1) * SUB)
                 cos_part, sin_part = turn_cos_sin_short(turns[rows])
-                turned[0, rows, :] = cos_part
-                turned[1, rows, :] = sin_part
+                turned[rows, 0:CHUNK] = cos_part
+                turned[rows, CHUNK : 2 * CHUNK] = sin_part
                 if chunk > 0 and sub == 0:
-                    update = contract_chunk(chunk - 1, 0)
-                if chunk > 0 and sub == pieces // 2 - 1:
-                    update = update + contract_chunk(chunk - 1, 1)
+                    update = contract_chunk(chunk - 1)
                     if chunk == 1:
                         acc[...] = update
                     else:
@@ -314,7 +287,7 @@
                 if chunk + 1 < chunks and sub == pieces - 2:
                     following = spread_turns(chunk + 1)
             turns = following
-        last = contract_chunk(chunks - 1, 0) + contract_chunk(chunks - 1, 1)
+        last = contract_chunk(chunks - 1)
         final = (acc[...] + last).astype(BF16)
 
         @pl.when(step == 0)
@@ -334,16 +307,12 @@
             def _():
                 models_in[me_d, span, :] = piece
 
-        @pl.when(step == 0)
-        def _():
-            lax.fori_loop(1, peers, send_coords, 0)
-
         return carry
 
     lax.fori_loop(0, pairs * gain_blocks, predict_step, 0)
-    coords_in[me_t] = coords_out[me_t]
-    index_copy.wait()
-    vis_copy.wait()
+    for fetch in fetches[5:]:
+        fetch.wait()
+
 
     ridge = jnp.broadcast_to(ridge_ref[...], (8, columns))
     lane = lax.broadcasted_iota(jnp.int32, (8, columns), 1)
@@ -432,6 +401,59 @@
             to = lax.rem(me_d + k, owners)
             resid_copy(me_d, part, to, to).start()
     resid[block_count] = jnp.zeros((BB, columns), BF16)
+
+    slot_lanes = block_row.shape[1]
+    tiles = jnp.broadcast_to(tile_ref[...], (slot_lanes, block_count))
+    named_tile = jnp.where(
+        lax.broadcasted_iota(jnp.int32, (slot_lanes, block_count), 0) == tiles, 1.0, 0.0
+    )
+    earlier = jnp.where(
+        lax.broadcasted_iota(jnp.int32, (block_count, block_count), 0)
+        < lax.broadcasted_iota(jnp.int32, (block_count, block_count), 1),
+        1.0,
+        0.0,
+    )
+    ranks = jnp.dot(named_tile.astype(BF16), earlier.astype(BF16), preferred_element_type=F32)
+    slot = jnp.sum(ranks * named_tile, axis=0, keepdims=True).astype(jnp.int32)
+    target = jnp.broadcast_to(tile_ref[...] * slots + slot, (slot_lanes, block_count))
+    lane = lax.broadcasted_iota(jnp.int32, (slot_lanes, block_count), 0)
+    taken = jnp.where(lane == target, 1.0, 0.0).astype(BF16)
+    block_id = lax.broadcasted_iota(jnp.int32, (8, block_count), 1) - block_count
+    picked = lax.dot_general(
+        block_id.astype(F32).astype(BF16),
+        taken,
+        (((1,), (1,)), ((), ())),
+        preferred_element_type=F32,
+    )
+    block_row[...] = picked[0:1, :].astype(jnp.int32) + block_count
+    index_copy = pltpu.make_async_copy(block_row, block_of_ref, local_sem.at[len(fetches)])
+    index_copy.start()
+
+    in_block = (
+        lax.broadcasted_iota(jnp.int32, (block_count, sample_rows), 1) // BB
+        == lax.broadcasted_iota(jnp.int32, (block_count, sample_rows), 0)
+    )
+    at_lane = jnp.where(
+        lax.broadcasted_iota(jnp.int32, (sample_rows, LANES), 0) % BB
+        == lax.broadcasted_iota(jnp.int32, (sample_rows, LANES), 1) % BB,
+        1.0,
+        0.0,
+    ).astype(BF16)
+    packed, side = coords_out.shape[1], coords_out.shape[1] // 2
+    spot = lax.broadcasted_iota(jnp.int32, (peers * packed, block_count), 0)
+    place_of = tile_ref[...] * packed + slot
+    sent = jnp.zeros((peers * packed, LANES), F32)
+    for which, row in enumerate((u_row, v_row)):
+        spread = jnp.where(in_block, jnp.broadcast_to(row, in_block.shape), 0.0).astype(BF16)
+        by_block = jnp.dot(spread, at_lane, preferred_element_type=F32).astype(BF16)
+        chosen = jnp.where(spot == place_of + which * side, 1.0, 0.0).astype(BF16)
+        sent = sent + jnp.dot(chosen, by_block, preferred_element_type=F32)
+    coords_out[...] = sent.astype(BF16).reshape(peers, packed, LANES)
+
+    lax.fori_loop(1, peers, send_coords, 0)
+    coords_in[me_t] = coords_out[me_t]
+    index_copy.wait()
+
     for part in range(gain_blocks):
         for k in range(1, owners):
             source = lax.rem(me_d + k, owners)
@@ -463,6 +485,13 @@
             device_id={"dir": partner},
             device_id_type=MESH,
         )
+
+    def paired(k):
+        other, bit = 0, 1
+        while bit < peers:
+            other = other + bit * ((me_t // bit + k // bit) % 2)
+            bit = 2 * bit
+        return other
 
     def dispatch(k, carry):
         to = lax.rem(me_t + k, peers)
@@ -531,7 +560,7 @@
     grid_sum = jnp.dot(tables[me_t], own_rows[...], preferred_element_type=F32)
 
     def source_at(k):
-        return lax.rem(me_t + peers - k, peers)
+        return paired(k)
 
     def arrive(k):
         source = source_at(k)
@@ -539,15 +568,16 @@
         hand_over(source, core).start()
 
     def add_source(k, total):
-        @pl.when(k + 1 < peers)
+        @pl.when(k + 3 < peers)
         def _():
-            arrive(k + 1)
+            arrive(k + 3)
 
         source = source_at(k)
         hand_over(source, 1 - core).wait_recv()
         return total + jnp.dot(tables[source], rows_in[source], preferred_element_type=F32)
 
-    arrive(1)
+    for ahead in range(1, min(3, peers - 1) + 1):
+        arrive(ahead)
     grid_sum = lax.fori_loop(1, peers, add_source, grid_sum)
     grid_ref[...] = (grid_sum * float(ROWS_DEV) ** (-0.5)).reshape(2, share, columns)
 
@@ -599,7 +629,6 @@
     group_rows = sample_rows // owners
     half_rows = slots // 2 * BB
     vmem = pl.BlockSpec(memory_space=pltpu.VMEM)
-    smem = pl.BlockSpec(memory_space=pltpu.SMEM)
     anywhere = pl.BlockSpec(memory_space=pl.ANY)
     dma = pltpu.SemaphoreType.DMA
     residual, subgrid = pl.pallas_call(
@@ -608,19 +637,25 @@
             pltpu.VMEM((sample_rows, columns), BF16),
             pltpu.VMEM((2, share, columns), F32),
         ),
-        in_specs=[vmem] * 5 + [smem] + [anywhere] * 2,
+        in_specs=[anywhere] * 8,
         out_specs=(vmem, vmem),
         scratch_shapes=[
+            pltpu.VMEM((2, comps), F32),
+            pltpu.VMEM((comps // LANES, LANES), jnp.int32),
+            pltpu.SMEM((DIR_DEV,), jnp.int32),
+            pltpu.VMEM((2, sample_rows), BF16),
+            pltpu.VMEM((2, comps, columns), BF16),
             pltpu.VMEM((group_rows, columns), BF16),
-            pltpu.VMEM((2, comps, columns), BF16),
-            pltpu.VMEM((2, comps, DIR_DEV * columns), BF16),
+            pltpu.VMEM((1, columns), F32),
+            pltpu.VMEM((1, block_count), jnp.int32),
+            pltpu.VMEM((2 * comps, DIR_DEV * columns), BF16),
             pltpu.VMEM((8, comps), BF16),
             pltpu.VMEM((sample_rows, 8), BF16),
             pltpu.VMEM((1, slot_lanes), jnp.int32),
             pltpu.SMEM((1, slot_lanes), jnp.int32),
             pltpu.VMEM((peers, packed, LANES), BF16),
-            pltpu.VMEM((2, 2 * GB, CHUNK), BF16),
-            pltpu.VMEM((2, 2 * GB, CHUNK), BF16),
+            pltpu.VMEM((2 * GB, 2 * CHUNK), BF16),
+            pltpu.VMEM((2 * GB, 2 * CHUNK), BF16),
             pltpu.VMEM((2 * GB, DIR_DEV * columns), F32),
             pltpu.VMEM((owners, group_rows, DIR_DEV * columns), BF16),
             pltpu.VMEM((owners, group_rows, DIR_DEV * columns), BF16),
@@ -640,20 +675,20 @@
             dma((peers,)),
             dma((peers,)),
             dma((peers,)),
-            dma((3,)),
+            dma((9,)),
         ],
         compiler_params=pltpu.CompilerParams(
             collective_id=0, has_side_effects=True, vmem_limit_bytes=60 * 1024 * 1024
         ),
     )(
+        comp_lm,
+        assignment.reshape(comps // LANES, LANES),
+        peel_order,
         uv_coords,
-        comp_lm,
+        spectra,
+        visibilities,
         ridge_weight[None, :],
-        assignment.reshape(comps // LANES, LANES),
         block_tile.reshape(1, block_count),
-        peel_order,
-        visibilities,
-        spectra,
     )
     residual, subgrid = pl.pallas_call(
         finish,

time: 34.8 us -> 31.7 us (0.911)
  the two profiles are of different devices: /device:TPU:0 before, /device:TPU:13 now
where the time goes in v3:
time: 31.7 us; the launch traced here: 31.2 us
  Pallas kernels  30.5 us (96%)
  between operations  0.64 us (2%)
    pallas_call x1, Pallas kernels, local(): pl.pallas_call(functools.partial(kernel, owners, peers, slots), out_shape...  29.7 us
    pallas_call x1, Pallas kernels, local(): pl.pallas_call(finish, out_shape=(jax.ShapeDtypeStruct(residual.shape, re...  0.81 us

profile of v3, /device:TPU:13, one launch (start us, length us, event | category | flops | bytes accessed | tf_op | source)
XLA Modules:
  0.0 31.2 jit_solution(4133114475339887667)
XLA Ops:
  0.6 29.7 %shard_map.95 = (bf16[1024,128]{1,0:T(8,128)(2,1)S(1)}, f32[2,256,128]{2,1,0:T(8,128)S(1)}) custom-call(f32[2,3072]{1,0:T(2,128)} %lm_hbm.1, s32[24,128]{1,0:T(8,128)} %bitcast.4, s32[3]{0:T(128)} %peel_hbm.1, bf16[2,1024]{1,0:T(2,128)(2,1)} %uv_hbm.1, bf16[2,3072,128]{2,1,0:T(8,128)(2,1)} %spec_hbm.1, bf16[1024,128]{1,0:T(8,128)(2,1)} %vis_hbm.1, ...), custom_call_target="tpu_custom_call" | custom-call | tf_op jit(solution)/shard_map/pallas_call | solution.py:634
  30.4 0.8 %shard_map.96 = (bf16[1024,128]{1,0:T(8,128)(2,1)}, f32[2,256,128]{2,1,0:T(8,128)}) custom-call(bf16[1024,128]{1,0:T(8,128)(2,1)S(1)} %get-tuple-element.6.resid_ref, f32[2,256,128]{2,1,0:T(8,128)S(1)} %get-tuple-element.7.grid_ref), custom_call_target="tpu_custom_call" | custom-call | tf_op jit(solution)/shard_map/pallas_call | solution.py:693

commit v4 on v3

--- a/solution.py
+++ b/solution.py
@@ -130,7 +130,8 @@
                 (entry_hbm, entry_ref),
                 (peel_hbm, peel_ref),
                 (uv_hbm, uv_ref),
-                (spec_hbm, spec_buf),
+                (spec_hbm.at[0], spec_buf.at[:, 0:columns]),
+                (spec_hbm.at[1], spec_buf.at[:, columns : 2 * columns]),
                 (own_part, vis_buf),
                 (ridge_hbm, ridge_ref),
                 (tile_hbm, tile_ref),
@@ -192,17 +193,16 @@
         at_low, at_high, (((1,), (1,)), ((), ())), preferred_element_type=F32
     )
     fetches[4].wait()
+    fetches[5].wait()
+    pair = 2 * columns
     for strip in range(strips):
-        own = jnp.broadcast_to(positions[:, strip : strip + 1], (LANES, columns)).astype(BF16)
-        span = pl.ds(strip * LANES, LANES)
-        chunk, inside = strip * LANES // CHUNK, strip * LANES % CHUNK
-        for part in range(2):
-            values = spec_buf[part, span, :]
-            target_span = pl.ds((2 * chunk + part) * CHUNK + inside, LANES)
-            for position in range(DIR_DEV):
-                masked[target_span, position * columns : (position + 1) * columns] = jnp.where(
-                    own == jnp.asarray(position, BF16), values, jnp.zeros_like(values)
-                )
+        own = jnp.broadcast_to(positions[:, strip : strip + 1], (LANES, pair)).astype(BF16)
+        span = slice(strip * LANES, (strip + 1) * LANES)
+        values = spec_buf[span, :]
+        for position in range(DIR_DEV):
+            masked[span, position * pair : (position + 1) * pair] = jnp.where(
+                own == jnp.asarray(position, BF16), values, jnp.zeros_like(values)
+            )
 
     def coords_copy(src, owner, to):
         return pltpu.make_async_remote_copy(
@@ -265,7 +265,23 @@
         def contract_chunk(chunk):
             return jnp.dot(
                 buffers[chunk % 2][...],
-                masked[2 * chunk * CHUNK : 2 * (chunk + 1) * CHUNK, :],
+                jnp.concatenate(
+                    [
+                        jnp.concatenate(
+                            [
+                                masked[
+                                    chunk * CHUNK : (chunk + 1) * CHUNK,
+                                    (2 * position + part) * columns : (2 * position + part + 1)
+                                    * columns,
+                                ]
+                                for position in range(DIR_DEV)
+                            ],
+                            axis=1,
+                        )
+                        for part in range(2)
+                    ],
+                    axis=0,
+                ),
                 preferred_element_type=F32,
             )
 
@@ -310,7 +326,7 @@
         return carry
 
     lax.fori_loop(0, pairs * gain_blocks, predict_step, 0)
-    for fetch in fetches[5:]:
+    for fetch in fetches[6:]:
         fetch.wait()
 
 
@@ -644,11 +660,11 @@
             pltpu.VMEM((comps // LANES, LANES), jnp.int32),
             pltpu.SMEM((DIR_DEV,), jnp.int32),
             pltpu.VMEM((2, sample_rows), BF16),
-            pltpu.VMEM((2, comps, columns), BF16),
+            pltpu.VMEM((comps, 2 * columns), BF16),
             pltpu.VMEM((group_rows, columns), BF16),
             pltpu.VMEM((1, columns), F32),
             pltpu.VMEM((1, block_count), jnp.int32),
-            pltpu.VMEM((2 * comps, DIR_DEV * columns), BF16),
+            pltpu.VMEM((comps, 2 * DIR_DEV * columns), BF16),
             pltpu.VMEM((8, comps), BF16),
             pltpu.VMEM((sample_rows, 8), BF16),
             pltpu.VMEM((1, slot_lanes), jnp.int32),
@@ -675,7 +691,7 @@
             dma((peers,)),
             dma((peers,)),
             dma((peers,)),
-            dma((9,)),
+            dma((10,)),
         ],
         compiler_params=pltpu.CompilerParams(
             collective_id=0, has_side_effects=True, vmem_limit_bytes=60 * 1024 * 1024

time: 31.7 us -> 31.4 us (level)
  no operation moved by 1% of the time
where the time goes in v4:
time: 31.4 us; the launch traced here: 30.9 us
  Pallas kernels  30.3 us (96%)
  between operations  0.64 us (2%)
    pallas_call x1, Pallas kernels, local(): pl.pallas_call(functools.partial(kernel, owners, peers, slots), out_shape...  29.5 us
    pallas_call x1, Pallas kernels, local(): pl.pallas_call(finish, out_shape=(jax.ShapeDtypeStruct(residual.shape, re...  0.81 us

profile of v4, /device:TPU:13, one launch (start us, length us, event | category | flops | bytes accessed | tf_op | source)
XLA Modules:
  0.0 30.9 jit_solution(7126818268743239469)
XLA Ops:
  0.6 29.5 %shard_map.95 = (bf16[1024,128]{1,0:T(8,128)(2,1)S(1)}, f32[2,256,128]{2,1,0:T(8,128)S(1)}) custom-call(f32[2,3072]{1,0:T(2,128)} %lm_hbm.1, s32[24,128]{1,0:T(8,128)} %bitcast.4, s32[3]{0:T(128)} %peel_hbm.1, bf16[2,1024]{1,0:T(2,128)(2,1)} %uv_hbm.1, bf16[2,3072,128]{2,1,0:T(8,128)(2,1)} %spec_hbm.1, bf16[1024,128]{1,0:T(8,128)(2,1)} %vis_hbm.1, ...), custom_call_target="tpu_custom_call" | custom-call | tf_op jit(solution)/shard_map/pallas_call | solution.py:650
  30.1 0.8 %shard_map.96 = (bf16[1024,128]{1,0:T(8,128)(2,1)}, f32[2,256,128]{2,1,0:T(8,128)}) custom-call(bf16[1024,128]{1,0:T(8,128)(2,1)S(1)} %get-tuple-element.6.resid_ref, f32[2,256,128]{2,1,0:T(8,128)S(1)} %get-tuple-element.7.grid_ref), custom_call_target="tpu_custom_call" | custom-call | tf_op jit(solution)/shard_map/pallas_call | solution.py:709

commit v5 on v4

--- a/solution.py
+++ b/solution.py
@@ -185,9 +185,10 @@
             value = value + jnp.where(peel_ref[position] == direction, position, 0)
         places.append(jnp.full((1, comps // DIR_DEV), value, jnp.int32))
     place = jnp.concatenate(places, axis=1).astype(F32)
-    low = lax.broadcasted_iota(jnp.int32, (LANES, comps), 0)
+    low = lax.broadcasted_iota(jnp.int32, (LANES, comps), 0).astype(F32).astype(BF16)
+    inside = (named % LANES).astype(F32).astype(BF16)
     high = lax.broadcasted_iota(jnp.int32, (padded, comps), 0)
-    at_low = jnp.where(low == named % LANES, 1.0, 0.0).astype(BF16)
+    at_low = jnp.where(low == inside, jnp.asarray(1, BF16), jnp.asarray(0, BF16))
     at_high = jnp.where(high == named // LANES, place, 0.0).astype(BF16)
     positions = lax.dot_general(
         at_low, at_high, (((1,), (1,)), ((), ())), preferred_element_type=F32
@@ -365,6 +366,7 @@
         return gain[0]
 
     per_gain = GB // BB
+    sublane = lax.broadcasted_iota(jnp.int32, (8, columns), 0)
 
     def peel_owner(part, owner, rest):
         models = [
@@ -377,11 +379,22 @@
             .reshape(GB // 8, 8, columns)
             for position in range(DIR_DEV)
         ]
+        power = over_rows(models[0] * models[0])
+        for position in range(1, DIR_DEV):
+            power = jnp.where(
+                sublane == position, over_rows(models[position] * models[position]), power
+            )
+        inverses = 1.0 / (power + ridge)
+        couples = moved(0.5 * ridge * inverses, reach)
+
+        def of_position(value, position):
+            return jnp.broadcast_to(value[position : position + 1, :], (8, columns))
+
         gains = []
         for position in range(DIR_DEV):
             model = models[position]
-            inverse = 1.0 / (over_rows(model * model) + ridge)
-            couple = moved(0.5 * ridge * inverse, reach)
+            inverse = of_position(inverses, position)
+            couple = {shift: of_position(couples[shift], position) for shift in couples}
             cross_sum = over_rows(rest * model)
             for before in range(position):
                 cross_sum = cross_sum - gains[before] * over_rows(models[before] * model)
@@ -584,15 +597,15 @@
         hand_over(source, core).start()
 
     def add_source(k, total):
-        @pl.when(k + 3 < peers)
+        @pl.when(k + 4 < peers)
         def _():
-            arrive(k + 3)
+            arrive(k + 4)
 
         source = source_at(k)
         hand_over(source, 1 - core).wait_recv()
         return total + jnp.dot(tables[source], rows_in[source], preferred_element_type=F32)
 
-    for ahead in range(1, min(3, peers - 1) + 1):
+    for ahead in range(1, min(4, peers - 1) + 1):
         arrive(ahead)
     grid_sum = lax.fori_loop(1, peers, add_source, grid_sum)
     grid_ref[...] = (grid_sum * float(ROWS_DEV) ** (-0.5)).reshape(2, share, columns)

time: 31.4 us -> 31.4 us (level)
  no operation moved by 1% of the time
where the time goes in v5:
time: 31.4 us; the launch traced here: 30.9 us
  Pallas kernels  30.3 us (96%)
  between operations  0.64 us (2%)
    pallas_call x1, Pallas kernels, local(): pl.pallas_call(functools.partial(kernel, owners, peers, slots), out_shape...  29.5 us
    pallas_call x1, Pallas kernels, local(): pl.pallas_call(finish, out_shape=(jax.ShapeDtypeStruct(residual.shape, re...  0.81 us

profile of v5, /device:TPU:13, one launch (start us, length us, event | category | flops | bytes accessed | tf_op | source)
XLA Modules:
  0.0 30.9 jit_solution(3661932367904724196)
XLA Ops:
  0.6 29.5 %shard_map.95 = (bf16[1024,128]{1,0:T(8,128)(2,1)S(1)}, f32[2,256,128]{2,1,0:T(8,128)S(1)}) custom-call(f32[2,3072]{1,0:T(2,128)} %lm_hbm.1, s32[24,128]{1,0:T(8,128)} %bitcast.4, s32[3]{0:T(128)} %peel_hbm.1, bf16[2,1024]{1,0:T(2,128)(2,1)} %uv_hbm.1, bf16[2,3072,128]{2,1,0:T(8,128)(2,1)} %spec_hbm.1, bf16[1024,128]{1,0:T(8,128)(2,1)} %vis_hbm.1, ...), custom_call_target="tpu_custom_call" | custom-call | tf_op jit(solution)/shard_map/pallas_call | solution.py:663
  30.1 0.8 %shard_map.96 = (bf16[1024,128]{1,0:T(8,128)(2,1)}, f32[2,256,128]{2,1,0:T(8,128)}) custom-call(bf16[1024,128]{1,0:T(8,128)(2,1)S(1)} %get-tuple-element.6.resid_ref, f32[2,256,128]{2,1,0:T(8,128)S(1)} %get-tuple-element.7.grid_ref), custom_call_target="tpu_custom_call" | custom-call | tf_op jit(solution)/shard_map/pallas_call | solution.py:722

commit v6 on v4

--- a/solution.py
+++ b/solution.py
@@ -584,15 +584,15 @@
         hand_over(source, core).start()
 
     def add_source(k, total):
-        @pl.when(k + 3 < peers)
+        @pl.when(k + 4 < peers)
         def _():
-            arrive(k + 3)
+            arrive(k + 4)
 
         source = source_at(k)
         hand_over(source, 1 - core).wait_recv()
         return total + jnp.dot(tables[source], rows_in[source], preferred_element_type=F32)
 
-    for ahead in range(1, min(3, peers - 1) + 1):
+    for ahead in range(1, min(4, peers - 1) + 1):
         arrive(ahead)
     grid_sum = lax.fori_loop(1, peers, add_source, grid_sum)
     grid_ref[...] = (grid_sum * float(ROWS_DEV) ** (-0.5)).reshape(2, share, columns)

time: 31.4 us -> 31.4 us (level)
  no operation moved by 1% of the time
where the time goes in v6:
time: 31.4 us; the launch traced here: 30.9 us
  Pallas kernels  30.3 us (96%)
  between operations  0.64 us (2%)
    pallas_call x1, Pallas kernels, local(): pl.pallas_call(functools.partial(kernel, owners, peers, slots), out_shape...  29.5 us
    pallas_call x1, Pallas kernels, local(): pl.pallas_call(finish, out_shape=(jax.ShapeDtypeStruct(residual.shape, re...  0.81 us

profile of v6, /device:TPU:13, one launch (start us, length us, event | category | flops | bytes accessed | tf_op | source)
XLA Modules:
  0.0 30.9 jit_solution(10522926190645485761)
XLA Ops:
  0.6 29.5 %shard_map.95 = (bf16[1024,128]{1,0:T(8,128)(2,1)S(1)}, f32[2,256,128]{2,1,0:T(8,128)S(1)}) custom-call(f32[2,3072]{1,0:T(2,128)} %lm_hbm.1, s32[24,128]{1,0:T(8,128)} %bitcast.4, s32[3]{0:T(128)} %peel_hbm.1, bf16[2,1024]{1,0:T(2,128)(2,1)} %uv_hbm.1, bf16[2,3072,128]{2,1,0:T(8,128)(2,1)} %spec_hbm.1, bf16[1024,128]{1,0:T(8,128)(2,1)} %vis_hbm.1, ...), custom_call_target="tpu_custom_call" | custom-call | tf_op jit(solution)/shard_map/pallas_call | solution.py:650
  30.1 0.8 %shard_map.96 = (bf16[1024,128]{1,0:T(8,128)(2,1)}, f32[2,256,128]{2,1,0:T(8,128)}) custom-call(bf16[1024,128]{1,0:T(8,128)(2,1)S(1)} %get-tuple-element.6.resid_ref, f32[2,256,128]{2,1,0:T(8,128)S(1)} %get-tuple-element.7.grid_ref), custom_call_target="tpu_custom_call" | custom-call | tf_op jit(solution)/shard_map/pallas_call | solution.py:709
